TPU v7x, 32 devices: a whole 2x2x4 slice. The times are simulated.
32 devices in a mesh: row: 8 (over y, x, core), col: 4 (over z).
Axes of the slice: x: 2, y: 2, z: 4, core: 2. Of those that a mesh axis runs over, the one named last changes fastest.
Arguments:
- pair: bfloat16 [256, 256, 128], P('row', 'col'), may hold values from -6 to 6
- cotangent: bfloat16 [256, 256, 128], P('row', 'col'), may hold values from -6 to 6
- length: int32 [1], replicated, may hold values from 128 to 256
- norm_gain: float32 [128], replicated, may hold values from 0.1 to 1.9
- norm_bias: float32 [128], replicated, may hold values from -1.5 to 1.5
- left_weight: bfloat16 [128, 256], replicated, may hold values from -0.5 to 0.5
- right_weight: bfloat16 [128, 256], replicated, may hold values from -0.5 to 0.5
- gate_weight: bfloat16 [128, 128], replicated, may hold values from -0.5 to 0.5
- out_gain: float32 [128], replicated, may hold values from 0.1 to 1.9
- out_bias: float32 [128], replicated, may hold values from -2 to 2
- out_weight: bfloat16 [128, 128], replicated, may hold values from -0.5 to 0.5
Outputs:
- update: bfloat16 [256, 256, 128], P('row', 'col')
- grad_pair: bfloat16 [256, 256, 128], P('row', 'col')
- grad_left: float32 [128, 256], replicated
- grad_right: float32 [128, 256], replicated
- grad_gating: float32 [128, 128], replicated
- grad_output: float32 [128, 128], replicated
- grad_norms: float32 [4, 128], replicated
Inputs may be any that keep to these rules, and one draw needn't show every extreme that they name: Tokens at positions 255 down to length are padding.
All inputs are finite; a program needn't handle non-finite values.
Results may differ from a plain program's by a relative error of at most 0.014.
Values may be sent and summed in bfloat16 or wider, within the bound.
No kernel may reach another device: no remote copies, remote signals or barrier semaphores. Data moves between devices by JAX's collectives and lax.ppermute only.
A program may use at most 128 MiB of HBM per device.

v0:
```python
import jax
import jax.numpy as jnp
from jax import lax
from jax.sharding import PartitionSpec as P

EPS = 1e-05


def broadcast(block, axis, holder):
    block = jnp.where(lax.axis_index(axis) == holder, block, jnp.zeros_like(block))
    return lax.psum(block, axis)


def normalize(values):
    center = values - jnp.mean(values, axis=-1, keepdims=True)
    inverse = lax.rsqrt(jnp.mean(center * center, axis=-1, keepdims=True) + EPS)
    return (center * inverse, inverse)


def gating(panel, weight, first_ok, second_ok, hidden):
    projected = jnp.einsum("ikc,ch->ikh", panel, weight, preferred_element_type=jnp.float32)
    values = projected[..., :hidden]
    sigmoid_val = jax.nn.sigmoid(projected[..., hidden:])
    pad_mask = (first_ok[:, None] & second_ok[None, :]).astype(jnp.float32)[..., None]
    return ((pad_mask * sigmoid_val * values).astype(jnp.bfloat16), values, sigmoid_val, pad_mask)


def push_back(partial_value, values, sigmoid_val, pad_mask, weight, panel):
    combined = jnp.concatenate(
        [
            partial_value * pad_mask * sigmoid_val,
            partial_value * pad_mask * values * sigmoid_val * (1.0 - sigmoid_val),
        ],
        axis=-1,
    ).astype(jnp.bfloat16)
    panel_grad = jnp.einsum("ikh,ch->ikc", combined, weight, preferred_element_type=jnp.float32)
    weight_grad = jnp.einsum("ikc,ikh->ch", panel, combined, preferred_element_type=jnp.float32)
    return (panel_grad, weight_grad)


def per_device(
    pair,
    cotangent,
    length,
    norm_gain,
    norm_bias,
    left_weight,
    right_weight,
    gate_weight,
    out_gain,
    out_bias,
    out_weight,
):
    row_index = lax.axis_index("row")
    col_index = lax.axis_index("col")
    n_row = lax.axis_size("row")
    n_col = lax.axis_size("col")
    per_col = n_row // n_col
    rows_dev = pair.shape[0]
    cols_dev = pair.shape[1]
    tokens = rows_dev * n_row
    hidden = out_weight.shape[0]
    pair_hat, pair_scale = normalize(pair.astype(jnp.float32))
    normed = (pair_hat * norm_gain + norm_bias).astype(jnp.bfloat16)
    real_count = length[0]
    second_ok = jnp.arange(tokens, dtype=jnp.int32) < real_count
    own_ok = row_index * rows_dev + jnp.arange(rows_dev, dtype=jnp.int32) < real_count
    partner_ok = col_index * cols_dev + jnp.arange(cols_dev, dtype=jnp.int32) < real_count
    left_tile, left_val, left_sig, tile_mask = gating(
        normed, left_weight, own_ok, partner_ok, hidden
    )
    right_tile, right_val, right_sig, unused_mask = gating(
        normed, right_weight, own_ok, partner_ok, hidden
    )
    row_panel = lax.all_gather(normed, "col", axis=1, tiled=True)
    pieces = []
    for member in range(per_col):
        pieces.append(broadcast(row_panel, "row", col_index * per_col + member))
    col_panel = jnp.concatenate(pieces, axis=0)
    left_act = gating(row_panel, left_weight, own_ok, second_ok, hidden)[0]
    right_act = gating(col_panel, right_weight, partner_ok, second_ok, hidden)[0]
    tri = jnp.einsum("ikh,jkh->ijh", left_act, right_act, preferred_element_type=jnp.float32)
    tri_hat, tri_scale = normalize(tri)
    tri_normed = (tri_hat * out_gain + out_bias).astype(jnp.bfloat16)
    outer_val = jnp.einsum(
        "ijh,hc->ijc", tri_normed, out_weight, preferred_element_type=jnp.float32
    )
    gate_val = jax.nn.sigmoid(
        jnp.einsum("ijc,cd->ijd", normed, gate_weight, preferred_element_type=jnp.float32)
    )
    update = (gate_val * outer_val).astype(jnp.bfloat16)
    upstream = cotangent.astype(jnp.float32)
    outer_grad = (upstream * gate_val).astype(jnp.bfloat16)
    gate_grad = (upstream * outer_val * gate_val * (1.0 - gate_val)).astype(jnp.bfloat16)
    grad_output = jnp.einsum(
        "ijh,ijc->hc", tri_normed, outer_grad, preferred_element_type=jnp.float32
    )
    grad_gating = jnp.einsum("ijc,ijd->cd", normed, gate_grad, preferred_element_type=jnp.float32)
    tnorm_grad = jnp.einsum(
        "ijc,hc->ijh", outer_grad, out_weight, preferred_element_type=jnp.float32
    )
    hat_grad = tnorm_grad * out_gain
    tri_grad = (
        tri_scale
        * (
            hat_grad
            - jnp.mean(hat_grad, axis=-1, keepdims=True)
            - tri_hat * jnp.mean(hat_grad * tri_hat, axis=-1, keepdims=True)
        )
    ).astype(jnp.bfloat16)
    row_partial = jnp.einsum(
        "ijh,jkh->ikh", tri_grad, right_act, preferred_element_type=jnp.float32
    )
    col_partial = jnp.einsum("ijh,ikh->jkh", tri_grad, left_act, preferred_element_type=jnp.float32)
    row_part = lax.psum_scatter(
        row_partial.astype(jnp.bfloat16), "col", scatter_dimension=1, tiled=True
    ).astype(jnp.float32)
    summed = lax.psum_scatter(
        col_partial.astype(jnp.bfloat16), "row", scatter_dimension=0, tiled=True
    )
    slab = summed[None]
    received = lax.all_to_all(slab, "col", split_axis=2, concat_axis=0, tiled=True)
    select = (jnp.arange(per_col, dtype=jnp.int32) == row_index // n_col).astype(jnp.bfloat16)
    spread = (received[:, None] * select[None, :, None, None, None]).reshape(
        (n_row,) + received.shape[1:]
    )
    returned = lax.all_to_all(spread, "row", split_axis=0, concat_axis=0, tiled=True)
    start = row_index % per_col * n_col
    owned = lax.dynamic_slice_in_dim(returned, start, n_col, 0).reshape(rows_dev, cols_dev, -1)
    col_part = owned.astype(jnp.float32)
    from_rows, grad_left = push_back(row_part, left_val, left_sig, tile_mask, left_weight, normed)
    from_cols, grad_right = push_back(
        col_part, right_val, right_sig, tile_mask, right_weight, normed
    )
    gate_back = jnp.einsum(
        "ijd,cd->ijc", gate_grad, gate_weight, preferred_element_type=jnp.float32
    )
    normed_grad = gate_back + from_rows + from_cols
    scaled = normed_grad * norm_gain
    grad_pair = (
        pair_scale
        * (
            scaled
            - jnp.mean(scaled, axis=-1, keepdims=True)
            - pair_hat * jnp.mean(scaled * pair_hat, axis=-1, keepdims=True)
        )
    ).astype(jnp.bfloat16)
    grad_norms = jnp.stack(
        [
            jnp.sum(normed_grad * pair_hat, axis=(0, 1)),
            jnp.sum(normed_grad, axis=(0, 1)),
            jnp.sum(tnorm_grad * tri_hat, axis=(0, 1)),
            jnp.sum(tnorm_grad, axis=(0, 1)),
        ]
    )
    totals = lax.psum((grad_left, grad_right, grad_gating, grad_output, grad_norms), ("row", "col"))
    inverse = 1.0 / tokens
    return (
        update,
        grad_pair,
        totals[0] * inverse,
        totals[1] * inverse,
        totals[2] * inverse,
        totals[3] * inverse,
        totals[4] * inverse,
    )


def solution(mesh):
    return jax.shard_map(
        per_device,
        mesh=mesh,
        in_specs=(
            P("row", "col", None),
            P("row", "col", None),
            P(),
            P(),
            P(),
            P(),
            P(),
            P(),
            P(),
            P(),
            P(),
        ),
        out_specs=(P("row", "col", None), P("row", "col", None), P(), P(), P(), P(), P()),
        check_vma=False,
    )
```

profile of v0, /device:TPU:0, one launch (start us, length us, event | category | flops | bytes accessed | tf_op | source)
XLA Modules:
  0.0 473.8 jit_solution(4896643660126480447)
XLA Ops:
  8.6 1.7 fusion.31
  10.3 2.5 fusion.25
  14.4 47.0 %all-gather.2.cloned.1.call-done = bf16[32,256,128]{2,1,0:T(8,128)(2,1)} async-done(((bf16[32,64,128]{2,1,0:T(8,128)(2,1)}), bf16[32,256,128]{2,1,0:T(8,128)(2,1)}) %all-gather.2.cloned.1.call-update) | async-done | bytes 2097168 | tf_op jit(solution)/shard_map/all_gather | solution.py:75
  61.4 3.8 broadcast_select_fusion.1
  68.3 3.1 copy.54
  71.5 2.8 fusion.53
  74.4 2.7 fusion.5
  77.0 4.6 copy.52
  81.6 63.4 %all-reduce.7.cloned.1.call-done = (bf16[32,256,128]{2,1,0:T(8,128)(2,1)}, bf16[32,256,128]{2,1,0:T(8,128)(2,1)}) async-done(((bf16[32,256,128]{2,1,0:T(8,128)(2,1)}, bf16[32,256,128]{2,1,0:T(8,128)(2,1)}), (bf16[32,256,128]{2,1,0:T(8,128)(2,1)}, bf16[32,256,128]{2,1,0:T(8,128)(2,1)})) %all-reduce.7.cloned.1.call-update) | async-done | bytes 4194320 | tf_op jit(solution)/shard_map/psum | solution.py:11
  145.1 4.5 fusion.10
  149.6 4.3 fusion
  154.0 6.8 %copy.51 = bf16[64,256,128]{1,0,2:T(8,128)(2,1)} copy(bf16[64,256,128]{2,1,0:T(8,128)(2,1)} %fusion) | data formatting | bytes 8388608 | tf_op jit(solution)/shard_map/convert_element_type | solution.py:25
  160.7 4.1 bitcast_reduce_fusion
  166.8 1.8 multiply_convert_fusion
  169.9 2.2 copy.66
  173.4 4.3 fusion.75
  177.7 4.6 copy.56
  182.5 41.1 %reduce-scatter.7.cloned.1.call-done = bf16[8,32768]{1,0:T(8,128)(2,1)} async-done(((bf16[64,32768]{1,0:T(8,128)(2,1)}), bf16[8,32768]{1,0:T(8,128)(2,1)}) %reduce-scatter.7.cloned.1.call-update) | async-done | bytes 524304
  226.4 4.6 all-to-all-start
  231.1 1.8 fusion.51
  232.9 1.7 fusion.56
  235.7 23.9 %all-to-all-done = bf16[1,8,256,128]{3,1,0,2:T(8,128)(2,1)} async-done(((bf16[1,8,256,128]{3,1,0,2:T(8,128)(2,1)}), bf16[1,8,256,128]{3,1,0,2:T(8,128)(2,1)}, u32[]{:S(2)}, u32[]{:S(2)}) %all-to-all-start) | async-done | bytes 524320 | tf_op jit(solution)/shard_map/all_to_all | solution.py:122
  261.9 4.2 all-to-all-start.1
  269.7 11.9 %all-to-all-done.1 = bf16[8,8,64,128]{3,2,1,0:T(8,128)(2,1)} async-done(((bf16[8,8,64,128]{3,2,1,0:T(8,128)(2,1)}), bf16[8,8,64,128]{3,2,1,0:T(8,128)(2,1)}, u32[]{:S(2)}, u32[]{:S(2)}) %all-to-all-start.1) | async-done | bytes 1048608 | tf_op jit(solution)/shard_map/all_to_all | solution.py:127
  282.7 2.8 fusion.49
  289.0 2.6 fusion.30
  291.6 37.2 %psum.55 = f32[4,128]{1,0:T(4,128)S(1)} all-reduce(f32[4,128]{1,0:T(4,128)S(1)} %pad_maximum_fusion.6), channel_id=1, replica_groups=mesh['row'=8,'col'=4] {'row','col'}, use_global_device_ids=true, to_apply=%region_20.21 | all-reduce | flops 512 | bytes 4096 | tf_op jit(solution)/shard_map/psum | solution.py:156
  328.8 1.9 fusion.29
  331.3 129.8 %all-reduce.5.cloned.1.call-done = (f32[128,256]{1,0:T(8,128)}, f32[128,256]{1,0:T(8,128)}, f32[128,128]{1,0:T(8,128)}, f32[128,128]{1,0:T(8,128)}) async-done(((f32[128,256]{1,0:T(8,128)}, f32[128,256]{1,0:T(8,128)}, f32[128,128]{1,0:T(8,128)}, f32[128,128]{1,0:T(8,128)}), (f32[128,256]{1,0:T(8,128)}, f32[128,256]{1,0:T(8,128)}, f32[128,128]{1,0:T(8,128)}, ...) | async-done | bytes 393232 | tf_op jit(solution)/shard_map/psum | solution.py:156
  461.2 1.6 broadcast_multiply_fusion
  462.7 1.6 broadcast_multiply_fusion.1
  464.3 1.5 broadcast_multiply_fusion.2
  (82 shorter events, 26.5 us)
Async XLA Ops:
  7.2 137.9 %copy-start = (bf16[128,256]{1,0:T(8,128)(2,1)S(1)}, bf16[128,256]{1,0:T(8,128)(2,1)}, u32[]{:S(2)}) copy-start(bf16[128,256]{1,0:T(8,128)(2,1)} %param.17) | copy-start | bytes 196612
  7.2 5.7 %copy-start.12 = (bf16[128,128]{1,0:T(8,128)(2,1)S(1)}, bf16[128,128]{1,0:T(8,128)(2,1)}, u32[]{:S(2)}) copy-start(bf16[128,128]{1,0:T(8,128)(2,1)} %param.18) | copy-start | bytes 98308
  7.2 54.2 %all-gather.2.cloned.1.call-start = ((), (), s32[]{:S(2)}) async-start(), calls=%async_computation.4 | async-start | bytes 2621440 | tf_op jit(solution)/shard_map/all_gather | solution.py:75
  12.8 132.2 %all-reduce.7.cloned.1.call-start = ((), (), s32[]{:S(2)}) async-start(), calls=%async_computation.8 | async-start | bytes 8388608 | tf_op jit(solution)/shard_map/psum | solution.py:11
  65.2 1.0 copy-start.6
  65.2 1.0 copy-start.11
  65.2 158.4 %reduce-scatter.7.cloned.1.call-start = ((), (), s32[]{:S(2)}) async-start(), calls=%async_computation.6 | async-start | bytes 4718592
  67.6 4.0 copy-start.9
  164.8 0.7 copy-start.14
  165.5 1.3 copy-start.15
  166.8 1.8 copy-start.1
  168.6 1.3 copy-start.3
  172.2 1.2 copy-start.4
  172.2 110.4 %reduce-scatter.5.cloned.1.call-start = ((), (), s32[]{:S(2)}) async-start(), calls=%async_computation.5 | async-start | bytes 2621440 | tf_op jit(solution)/shard_map/reduce_scatter | solution.py:115
  223.6 7.5 %copy-start.2 = (bf16[32,64,128]{2,1,0:T(8,128)(2,1)S(1)}, bf16[32,64,128]{2,1,0:T(8,128)(2,1)}, u32[]{:S(2)}) copy-start(bf16[32,64,128]{2,1,0:T(8,128)(2,1)} %fusion.25) | copy-start | bytes 1572868
  226.4 33.2 %all-to-all-start = ((bf16[1,8,256,128]{3,1,0,2:T(8,128)(2,1)}), bf16[1,8,256,128]{3,1,0,2:T(8,128)(2,1)}, u32[]{:S(2)}, u32[]{:S(2)}) async-start(bf16[1,8,256,128]{3,1,0,2:T(8,128)(2,1)} %copy.58), calls=%async_computation.1 | async-start | bytes 1048576 | tf_op jit(solution)/shard_map/all_to_all | solution.py:122
  231.1 3.5 copy-start.8
  260.8 5.4 %copy-start.7 = (bf16[32,64,128]{2,1,0:T(8,128)(2,1)S(1)}, bf16[32,64,128]{2,1,0:T(8,128)(2,1)}, u32[]{:S(2)}) copy-start(bf16[32,64,128]{2,1,0:T(8,128)(2,1)} %param.12) | copy-start | bytes 1572868
  261.9 19.6 %all-to-all-start.1 = ((bf16[8,8,64,128]{3,2,1,0:T(8,128)(2,1)}), bf16[8,8,64,128]{3,2,1,0:T(8,128)(2,1)}, u32[]{:S(2)}, u32[]{:S(2)}) async-start(bf16[8,8,64,128]{3,2,1,0:T(8,128)(2,1)} %bitcast_multiply_fusion), calls=%async_computation.2 | async-start | bytes 2097152 | tf_op jit(solution)/shard_map/all_to_all | solution.py:127
  266.2 195.0 %all-reduce.5.cloned.1.call-start = ((), (), s32[]{:S(2)}) async-start(), calls=%async_computation.7 | async-start | bytes 786432 | tf_op jit(solution)/shard_map/psum | solution.py:156
  285.5 2.5 copy-start.10
  286.5 2.5 copy-start.5
  286.5 2.5 copy-start.13
Sparse Core Ops, SparseCore 0:
  13.0 48.3 all-gather.1
  65.4 79.6 all-reduce.6
  172.3 51.2 reduce-scatter.6
  225.7 51.5 reduce-scatter.4
  330.9 130.2 all-reduce.4
where the time goes:
time: 475 us; the launch traced here: 474 us
  waiting for transfers between devices  317 us (67%)
  blocking collectives  37.2 us (8%)
  matrix products  32.8 us (7%)
  other arithmetic  32.6 us (7%)
  local copies, waits for them, and re-layouts  29.7 us (6%)
  between operations  14.8 us (3%)
  starting transfers between devices  9.43 us (2%)
    psum x1, waiting for transfers between devices, per_device(): lax.psum((grad_left, grad_right, grad_gating, grad_output, grad_norms), (...  130 us
    psum x1, waiting for transfers between devices, broadcast(): return lax.psum(block, axis)  63.4 us
    all_gather x1, waiting for transfers between devices, per_device(): row_panel = lax.all_gather(normed, 'col', axis=1, tiled=True)  47 us
    unnamed x6, waiting for transfers between devices  41.2 us
    psum x1, blocking collectives, per_device(): lax.psum((grad_left, grad_right, grad_gating, grad_output, grad_norms), (...  37.2 us
    all_to_all x1, waiting for transfers between devices, per_device(): lax.all_to_all(slab, 'col', split_axis=2, concat_axis=0, tiled=True)  23.9 us
    all_to_all x1, waiting for transfers between devices, per_device(): lax.all_to_all(spread, 'row', split_axis=0, concat_axis=0, tiled=True)  11.9 us
    convert_element_type x2, local copies, waits for them, and re-layouts, gating(): (pad_mask * sigmoid_val * values).astype(jnp.bfloat16)  11.4 us
  transfers between devices with their start and end apart: 7, of which 6 were waited for; matrix products, arithmetic and copies ran while one was open for 8% of the time, Pallas kernels for 0%

commit v1 on v0

--- a/solution.py
+++ b/solution.py
@@ -153,7 +153,9 @@
             jnp.sum(tnorm_grad, axis=(0, 1)),
         ]
     )
-    totals = lax.psum((grad_left, grad_right, grad_gating, grad_output, grad_norms), ("row", "col"))
+    totals = lax.psum(
+        lax.psum((grad_left, grad_right, grad_gating, grad_output, grad_norms), "row"), "col"
+    )
     inverse = 1.0 / tokens
     return (
         update,

time: 475 us -> 419 us (0.88)
  waiting for transfers between devices: 317 us -> 276 us
  blocking collectives: 37.2 us -> 22.1 us
    psum x1 -> x2, waiting for transfers between devices: 130 us -> 88.7 us  [the longest x1 52.4 us: per_device(): lax.psum((grad_left, grad_right, grad_gating, grad_output, grad_norms), '...]
    psum x1 -> x2, blocking collectives: 37.2 us -> 22.1 us  [the longest x1 11.8 us: per_device(): lax.psum((grad_left, grad_right, grad_gating, grad_output, grad_norms), '...]
    unnamed x6 -> x7, waiting for transfers between devices: 41.2 us -> 41.2 us
  transfers between devices with their start and end apart: 7 -> 8, of which waited for: 6 -> 7; matrix products, arithmetic and copies ran while one was open for 8% -> 10% of each run, Pallas kernels for 0% -> 0%
where the time goes in v1:
time: 419 us; the launch traced here: 418 us
  waiting for transfers between devices  276 us (66%)
  matrix products  32.8 us (8%)
  other arithmetic  32.6 us (8%)
  local copies, waits for them, and re-layouts  29.7 us (7%)
  blocking collectives  22.1 us (5%)
  between operations  15.1 us (4%)
  starting transfers between devices  9.47 us (2%)
    psum x1, waiting for transfers between devices, broadcast(): return lax.psum(block, axis)  63.4 us
    psum x1, waiting for transfers between devices, per_device(): lax.psum((grad_left, grad_right, grad_gating, grad_output, grad_norms), '...  52.4 us
    all_gather x1, waiting for transfers between devices, per_device(): row_panel = lax.all_gather(normed, 'col', axis=1, tiled=True)  47 us
    unnamed x7, waiting for transfers between devices  41.2 us
    psum x1, waiting for transfers between devices, per_device(): lax.psum(lax.psum((grad_left, grad_right, grad_gating, grad_output, grad_...  36.3 us
    all_to_all x1, waiting for transfers between devices, per_device(): lax.all_to_all(slab, 'col', split_axis=2, concat_axis=0, tiled=True)  23.9 us
    all_to_all x1, waiting for transfers between devices, per_device(): lax.all_to_all(spread, 'row', split_axis=0, concat_axis=0, tiled=True)  11.9 us
    psum x1, blocking collectives, per_device(): lax.psum((grad_left, grad_right, grad_gating, grad_output, grad_norms), '...  11.8 us
  transfers between devices with their start and end apart: 8, of which 7 were waited for; matrix products, arithmetic and copies ran while one was open for 10% of the time, Pallas kernels for 0%

profile of v1, /device:TPU:0, one launch (start us, length us, event | category | flops | bytes accessed | tf_op | source)
XLA Modules:
  0.0 417.9 jit_solution(13426788526660204223)
XLA Ops:
  8.6 1.7 fusion.31
  10.3 2.5 fusion.25
  14.4 47.0 %all-gather.2.cloned.1.call-done = bf16[32,256,128]{2,1,0:T(8,128)(2,1)} async-done(((bf16[32,64,128]{2,1,0:T(8,128)(2,1)}), bf16[32,256,128]{2,1,0:T(8,128)(2,1)}) %all-gather.2.cloned.1.call-update) | async-done | bytes 2097168 | tf_op jit(solution)/shard_map/all_gather | solution.py:75
  61.4 3.8 broadcast_select_fusion.1
  68.3 3.1 copy.54
  71.5 2.8 fusion.53
  74.4 2.7 fusion.5
  77.0 4.6 %copy.52 = bf16[32,256,128]{1,0,2:T(8,128)(2,1)} copy(bf16[32,256,128]{2,1,0:T(8,128)(2,1)} %fusion.5) | data formatting | bytes 4194304 | tf_op jit(solution)/shard_map/convert_element_type | solution.py:25
  81.6 63.4 %all-reduce.11.cloned.1.call-done = (bf16[32,256,128]{2,1,0:T(8,128)(2,1)}, bf16[32,256,128]{2,1,0:T(8,128)(2,1)}) async-done(((bf16[32,256,128]{2,1,0:T(8,128)(2,1)}, bf16[32,256,128]{2,1,0:T(8,128)(2,1)}), (bf16[32,256,128]{2,1,0:T(8,128)(2,1)}, bf16[32,256,128]{2,1,0:T(8,128)(2,1)})) %all-reduce.11.cloned.1.call-update) | async-done | bytes 4194320 | tf_op jit(solution)/shard_map/psum | solution.py:11
  145.1 4.5 %fusion.10 = f32[64,256,256]{2,1,0:T(8,128)S(1)} fusion(bf16[32,256,128]{2,1,0:T(8,128)(2,1)} %get-tuple-element.22, bf16[32,256,128]{2,1,0:T(8,128)(2,1)} %get-tuple-element.23, bf16[128,256]{1,0:T(8,128)(2,1)S(1)} %copy-done), kind=kOutput, calls=%fused_computation.14 | convolution fusion | flops 1075838976 | bytes 21037056 | tf_op jit(solution)/shard_map/ikc,ch->ikh/dot_general | solution.py:21
  149.6 4.3 %fusion = bf16[64,256,128]{2,1,0:T(8,128)(2,1)} fusion(f32[64,256,256]{2,1,0:T(8,128)S(1)} %fusion.10, f32[64,256]{1,0:T(8,128)S(1)} %and_convert_fusion), kind=kLoop, calls=%fused_computation.1 | loop fusion | flops 12582912 | bytes 21037056 | tf_op jit(solution)/shard_map/convert_element_type | solution.py:25
  154.0 6.8 %copy.51 = bf16[64,256,128]{1,0,2:T(8,128)(2,1)} copy(bf16[64,256,128]{2,1,0:T(8,128)(2,1)} %fusion) | data formatting | bytes 8388608 | tf_op jit(solution)/shard_map/convert_element_type | solution.py:25
  160.7 4.1 bitcast_reduce_fusion
  166.8 1.8 multiply_convert_fusion
  169.9 2.2 copy.66
  173.4 4.3 %fusion.75 = bf16[128,256,32]{1,2,0:T(8,128)(2,1)} fusion(bf16[32,64,128]{1,0,2:T(8,128)(2,1)S(1)} %copy-done.4, bf16[64,256,128]{1,0,2:T(8,128)(2,1)} %copy.51), kind=kOutput, calls=%fused_computation.136 | convolution fusion | flops 134217728 | bytes 6815744 | tf_op jit(solution)/shard_map/ijh,jkh->ikh/dot_general | solution.py:111
  177.7 4.6 %copy.56 = bf16[128,256,32]{0,1,2:T(8,128)(2,1)} copy(bf16[128,256,32]{1,2,0:T(8,128)(2,1)} %fusion.75) | data formatting | bytes 4194304 | tf_op jit(solution)/shard_map/ijh,jkh->ikh/dot_general | solution.py:111
  182.5 41.1 %reduce-scatter.7.cloned.1.call-done = bf16[8,32768]{1,0:T(8,128)(2,1)} async-done(((bf16[64,32768]{1,0:T(8,128)(2,1)}), bf16[8,32768]{1,0:T(8,128)(2,1)}) %reduce-scatter.7.cloned.1.call-update) | async-done | bytes 524304
  226.4 4.6 %all-to-all-start = ((bf16[1,8,256,128]{3,1,0,2:T(8,128)(2,1)}), bf16[1,8,256,128]{3,1,0,2:T(8,128)(2,1)}, u32[]{:S(2)}, u32[]{:S(2)}) async-start(bf16[1,8,256,128]{3,1,0,2:T(8,128)(2,1)} %copy.58), calls=%async_computation.1 | async-start | bytes 1048576 | tf_op jit(solution)/shard_map/all_to_all | solution.py:122
  231.1 1.8 fusion.51
  232.9 1.7 fusion.56
  235.7 23.9 %all-to-all-done = bf16[1,8,256,128]{3,1,0,2:T(8,128)(2,1)} async-done(((bf16[1,8,256,128]{3,1,0,2:T(8,128)(2,1)}), bf16[1,8,256,128]{3,1,0,2:T(8,128)(2,1)}, u32[]{:S(2)}, u32[]{:S(2)}) %all-to-all-start) | async-done | bytes 524320 | tf_op jit(solution)/shard_map/all_to_all | solution.py:122
  261.9 4.2 %all-to-all-start.1 = ((bf16[8,8,64,128]{3,2,1,0:T(8,128)(2,1)}), bf16[8,8,64,128]{3,2,1,0:T(8,128)(2,1)}, u32[]{:S(2)}, u32[]{:S(2)}) async-start(bf16[8,8,64,128]{3,2,1,0:T(8,128)(2,1)} %bitcast_multiply_fusion), calls=%async_computation.2 | async-start | bytes 2097152 | tf_op jit(solution)/shard_map/all_to_all | solution.py:127
  269.7 11.9 %all-to-all-done.1 = bf16[8,8,64,128]{3,2,1,0:T(8,128)(2,1)} async-done(((bf16[8,8,64,128]{3,2,1,0:T(8,128)(2,1)}), bf16[8,8,64,128]{3,2,1,0:T(8,128)(2,1)}, u32[]{:S(2)}, u32[]{:S(2)}) %all-to-all-start.1) | async-done | bytes 1048608 | tf_op jit(solution)/shard_map/all_to_all | solution.py:127
  282.7 2.8 fusion.49
  289.0 2.6 fusion.30
  291.6 11.8 %psum.94 = f32[4,128]{1,0:T(4,128)S(1)} all-reduce(f32[4,128]{1,0:T(4,128)S(1)} %pad_maximum_fusion.6), channel_id=1, replica_groups=mesh['row'=8,'col'=4] {'row'}, use_global_device_ids=true, to_apply=%region_24.25 | all-reduce | flops 512 | bytes 4096 | tf_op jit(solution)/shard_map/psum | solution.py:157
  303.4 10.3 %psum.95 = f32[4,128]{1,0:T(4,128)S(1)} all-reduce(f32[4,128]{1,0:T(4,128)S(1)} %psum.94), channel_id=1, replica_groups=mesh['row'=8,'col'=4] {'col'}, use_global_device_ids=true, to_apply=%region_25.26 | all-reduce | flops 512 | bytes 4096 | tf_op jit(solution)/shard_map/psum | solution.py:156
  313.7 52.4 %all-reduce.7.cloned.1.call-done = (f32[128,256]{1,0:T(8,128)}, f32[128,256]{1,0:T(8,128)}, f32[128,128]{1,0:T(8,128)}, f32[128,128]{1,0:T(8,128)}) async-done(((f32[128,256]{1,0:T(8,128)}, f32[128,256]{1,0:T(8,128)}, f32[128,128]{1,0:T(8,128)}, f32[128,128]{1,0:T(8,128)}), (f32[128,256]{1,0:T(8,128)}, f32[128,256]{1,0:T(8,128)}, f32[128,128]{1,0:T(8,128)}, ...) | async-done | bytes 393232 | tf_op jit(solution)/shard_map/psum | solution.py:157
  366.7 1.9 fusion.29
  368.6 36.3 %all-reduce.9.cloned.1.call-done = (f32[128,256]{1,0:T(8,128)}, f32[128,256]{1,0:T(8,128)}, f32[128,128]{1,0:T(8,128)}, f32[128,128]{1,0:T(8,128)}) async-done(((f32[128,256]{1,0:T(8,128)}, f32[128,256]{1,0:T(8,128)}, f32[128,128]{1,0:T(8,128)}, f32[128,128]{1,0:T(8,128)}), (f32[128,256]{1,0:T(8,128)}, f32[128,256]{1,0:T(8,128)}, f32[128,128]{1,0:T(8,128)}, ...) | async-done | bytes 393232 | tf_op jit(solution)/shard_map/psum | solution.py:156
  404.9 1.6 broadcast_multiply_fusion
  (86 shorter events, 29.6 us)
Async XLA Ops:
  7.2 137.9 %copy-start = (bf16[128,256]{1,0:T(8,128)(2,1)S(1)}, bf16[128,256]{1,0:T(8,128)(2,1)}, u32[]{:S(2)}) copy-start(bf16[128,256]{1,0:T(8,128)(2,1)} %param.17) | copy-start | bytes 196612
  7.2 5.7 %copy-start.12 = (bf16[128,128]{1,0:T(8,128)(2,1)S(1)}, bf16[128,128]{1,0:T(8,128)(2,1)}, u32[]{:S(2)}) copy-start(bf16[128,128]{1,0:T(8,128)(2,1)} %param.18) | copy-start | bytes 98308
  7.2 54.2 %all-gather.2.cloned.1.call-start = ((), (), s32[]{:S(2)}) async-start(), calls=%async_computation.4 | async-start | bytes 2621440 | tf_op jit(solution)/shard_map/all_gather | solution.py:75
  12.8 132.2 %all-reduce.11.cloned.1.call-start = ((), (), s32[]{:S(2)}) async-start(), calls=%async_computation.9 | async-start | bytes 8388608 | tf_op jit(solution)/shard_map/psum | solution.py:11
  65.2 1.0 copy-start.6
  65.2 1.0 copy-start.11
  65.2 158.4 %reduce-scatter.7.cloned.1.call-start = ((), (), s32[]{:S(2)}) async-start(), calls=%async_computation.6 | async-start | bytes 4718592
  67.6 4.0 copy-start.9
  164.8 0.7 copy-start.14
  165.5 1.3 copy-start.15
  166.8 1.8 copy-start.1
  168.6 1.3 copy-start.3
  172.2 1.2 copy-start.4
  172.2 110.4 %reduce-scatter.5.cloned.1.call-start = ((), (), s32[]{:S(2)}) async-start(), calls=%async_computation.5 | async-start | bytes 2621440 | tf_op jit(solution)/shard_map/reduce_scatter | solution.py:115
  223.6 7.5 %copy-start.2 = (bf16[32,64,128]{2,1,0:T(8,128)(2,1)S(1)}, bf16[32,64,128]{2,1,0:T(8,128)(2,1)}, u32[]{:S(2)}) copy-start(bf16[32,64,128]{2,1,0:T(8,128)(2,1)} %fusion.25) | copy-start | bytes 1572868
  226.4 33.2 %all-to-all-start = ((bf16[1,8,256,128]{3,1,0,2:T(8,128)(2,1)}), bf16[1,8,256,128]{3,1,0,2:T(8,128)(2,1)}, u32[]{:S(2)}, u32[]{:S(2)}) async-start(bf16[1,8,256,128]{3,1,0,2:T(8,128)(2,1)} %copy.58), calls=%async_computation.1 | async-start | bytes 1048576 | tf_op jit(solution)/shard_map/all_to_all | solution.py:122
  231.1 3.5 copy-start.8
  260.8 5.4 %copy-start.7 = (bf16[32,64,128]{2,1,0:T(8,128)(2,1)S(1)}, bf16[32,64,128]{2,1,0:T(8,128)(2,1)}, u32[]{:S(2)}) copy-start(bf16[32,64,128]{2,1,0:T(8,128)(2,1)} %param.12) | copy-start | bytes 1572868
  261.9 19.6 %all-to-all-start.1 = ((bf16[8,8,64,128]{3,2,1,0:T(8,128)(2,1)}), bf16[8,8,64,128]{3,2,1,0:T(8,128)(2,1)}, u32[]{:S(2)}, u32[]{:S(2)}) async-start(bf16[8,8,64,128]{3,2,1,0:T(8,128)(2,1)} %bitcast_multiply_fusion), calls=%async_computation.2 | async-start | bytes 2097152 | tf_op jit(solution)/shard_map/all_to_all | solution.py:127
  266.2 99.9 %all-reduce.7.cloned.1.call-start = ((), (), s32[]{:S(2)}) async-start(), calls=%async_computation.7 | async-start | bytes 786432 | tf_op jit(solution)/shard_map/psum | solution.py:157
  285.5 2.5 copy-start.10
  286.5 2.5 copy-start.5
  286.5 2.5 copy-start.13
  313.6 91.3 %all-reduce.9.cloned.1.call-start = ((), (), s32[]{:S(2)}) async-start(), calls=%async_computation.8 | async-start | bytes 786432 | tf_op jit(solution)/shard_map/psum | solution.py:156
Sparse Core Ops, SparseCore 0:
  13.0 48.3 all-gather.1
  65.4 79.6 all-reduce.10
  172.3 51.2 reduce-scatter.6
  225.7 51.5 reduce-scatter.4
  313.8 52.2 all-reduce.6
  368.6 36.3 all-reduce.8
